TPU v7x, 128 devices: a whole 4x4x4 slice. The times are simulated.
128 devices in a mesh: ia: 4 (over x_lo, core), ja: 16 (over y, z), ka: 2 (over x_hi).
Axes of the slice: x: 4 (x_hi: 2, x_lo: 2; x = x_hi * 2 + x_lo), y: 4, z: 4, core: 2. Of those that a mesh axis runs over, the one named last changes fastest.
Arguments:
- tensor: bfloat16 [768, 1024, 256], P('ia', 'ja', 'ka'), may hold values from -190 to 190
- matrix: bfloat16 [768, 16384], P('ia', ('ja', 'ka')), may hold values from -160 to 160
- second_in: float32 [1024, 256], P('ja'), may hold values from -10 to 10
- third_in: float32 [256, 256], P('ka'), may hold values from -10 to 10
- column_in: float32 [16384, 256], P(('ja', 'ka')), may hold values from -510 to 510
Outputs:
- first_out: float32 [768, 256], P(('ia', 'ja', 'ka'))
- second_out: float32 [16, 64, 256], P('ja', ('ia', 'ka'))
- third_out: float32 [2, 128, 256], P('ka', ('ia', 'ja'))
- column_out: float32 [32, 512, 256], P(('ja', 'ka'), 'ia')
All inputs are finite; a program needn't handle non-finite values.
Results may differ from a plain program's by a relative error of at most 0.02.
Values may be sent and summed in bfloat16 or wider, within the bound.
No kernel may reach another device: no remote copies, remote signals or barrier semaphores. Data moves between devices by JAX's collectives and lax.ppermute only.
A program may use at most 64 MiB of HBM per device.

v0:
```python
import jax
import jax.numpy as jnp
from jax import lax
from jax.sharding import PartitionSpec as P


def gram_of(factor):
    return jnp.dot(
        factor.T, factor, precision=lax.Precision.HIGHEST, preferred_element_type=jnp.float32
    )


def solve_rows(right_side, system):
    lower_factor = jnp.linalg.cholesky(system)
    return jax.scipy.linalg.cho_solve((lower_factor, True), right_side.T).T


def column_norms(unscaled, row_total):
    squares = lax.psum(jnp.sum(unscaled * unscaled, axis=0), ("ia", "ja", "ka"))
    return lax.rsqrt(squares / row_total + 1e-06)


def normalize(unscaled, row_total, want_gram):
    if want_gram:
        scaled = unscaled * column_norms(unscaled, row_total)
        return (scaled, lax.psum(gram_of(scaled), ("ia", "ja", "ka")))
    return (unscaled * column_norms(unscaled, row_total), None)


def body(tensor, matrix, second_in, third_in, column_in):
    span_first, span_second, span_third = tensor.shape
    span_column = matrix.shape[1]
    rank_width = second_in.shape[1]
    total_first = span_first * lax.axis_size("ia")
    total_second = span_second * lax.axis_size("ja")
    total_third = span_third * lax.axis_size("ka")
    total_column = span_column * lax.axis_size("ja") * lax.axis_size("ka")
    gram_second = lax.psum(gram_of(second_in), "ja")
    gram_third = lax.psum(gram_of(third_in), "ka")
    gram_column = lax.psum(gram_of(column_in), ("ja", "ka"))
    column_half = column_in.astype(jnp.bfloat16)
    weights_one = (second_in[:, None, :] * third_in[None, :, :]).astype(jnp.bfloat16)
    first_whole = lax.dot_general(
        tensor, weights_one, (((1, 2), (0, 1)), ((), ())), preferred_element_type=jnp.float32
    )
    first_whole = first_whole + jnp.dot(matrix, column_half, preferred_element_type=jnp.float32)
    system_one = gram_second * gram_third + gram_column
    partial_rows = lax.psum_scatter(first_whole, ("ja", "ka"), scatter_dimension=0, tiled=True)
    first_new, gram_first = normalize(solve_rows(partial_rows, system_one), total_first, True)
    first_half = lax.all_gather(first_new.astype(jnp.bfloat16), ("ja", "ka"), axis=0, tiled=True)
    weights_two = (first_half.astype(jnp.float32)[:, None, :] * third_in[None, :, :]).astype(
        jnp.bfloat16
    )
    second_whole = lax.dot_general(
        tensor, weights_two, (((0, 2), (0, 1)), ((), ())), preferred_element_type=jnp.float32
    )
    partial_second = lax.psum_scatter(second_whole, ("ia", "ka"), scatter_dimension=0, tiled=True)
    second_new, gram_updated = normalize(
        solve_rows(partial_second, gram_first * gram_third), total_second, True
    )
    second_half = lax.all_gather(second_new.astype(jnp.bfloat16), ("ia", "ka"), axis=0, tiled=True)
    weights_three = (first_half[:, None, :] * second_half[None, :, :]).reshape(
        span_first * span_second, rank_width
    )
    tensor_flat = tensor.reshape(span_first * span_second, span_third)
    third_whole = lax.dot_general(
        tensor_flat, weights_three, (((0,), (0,)), ((), ())), preferred_element_type=jnp.float32
    )
    partial_third = lax.psum_scatter(third_whole, ("ia", "ja"), scatter_dimension=0, tiled=True)
    third_new, unused_third = normalize(
        solve_rows(partial_third, gram_first * gram_updated), total_third, False
    )
    column_whole = lax.dot_general(
        matrix, first_half, (((0,), (0,)), ((), ())), preferred_element_type=jnp.float32
    )
    partial_column = lax.psum_scatter(column_whole, "ia", scatter_dimension=0, tiled=True)
    column_new, unused_column = normalize(
        solve_rows(partial_column, gram_first), total_column, False
    )
    return (first_new, second_new[None], third_new[None], column_new[None])


def solution(mesh):
    placed = (
        P("ia", "ja", "ka"),
        P("ia", ("ja", "ka")),
        P("ja", None),
        P("ka", None),
        P(("ja", "ka"), None),
    )
    return jax.shard_map(
        body,
        mesh=mesh,
        in_specs=placed,
        out_specs=(
            P(("ia", "ja", "ka"), None),
            P("ja", ("ia", "ka"), None),
            P("ka", ("ia", "ja"), None),
            P(("ja", "ka"), "ia", None),
        ),
        check_vma=False,
    )
```

profile of v0, /device:TPU:1, one launch (start us, length us, event | category | flops | bytes accessed | tf_op | source)
XLA Modules:
  0.0 1613.4 jit_solution(9190007200172320423)
XLA Ops:
  18.8 86.8 %fusion = f32[8,256]{1,0:T(8,128)S(1)} fusion(f32[192,256]{1,0:T(8,128)S(1)} %convolution_add_fusion), kind=kCustom, calls=%all-reduce-scatter | all-reduce-scatter fusion | flops 65537 | bytes 205312
  132.0 211.0 %all-reduce.16.cloned.1.call-done = f32[256,256]{0,1:T(8,128)} async-done(((f32[256,256]{0,1:T(8,128)}), f32[256,256]{0,1:T(8,128)}) %all-reduce.16.cloned.1.call-update) | async-done | bytes 262160 | tf_op jit(solution)/shard_map/psum | solution.py:40
  343.1 109.3 %all-reduce.12.cloned.1.call-done = f32[256,256]{0,1:T(8,128)} async-done(((f32[256,256]{0,1:T(8,128)}), f32[256,256]{0,1:T(8,128)}) %all-reduce.12.cloned.1.call-update) | async-done | bytes 262160 | tf_op jit(solution)/shard_map/psum | solution.py:38
  452.3 34.5 %all-reduce.14.cloned.1.call-done = f32[256,256]{0,1:T(8,128)} async-done(((f32[256,256]{0,1:T(8,128)}), f32[256,256]{0,1:T(8,128)}) %all-reduce.14.cloned.1.call-update) | async-done | bytes 262160 | tf_op jit(solution)/shard_map/psum | solution.py:39
  488.2 11.7 cholesky.214
  510.3 11.7 cholesky.231
  528.1 20.2 %custom-call.36 = f32[2,128,128]{1,2,0:T(8,128)S(1)} custom-call(f32[2,128,128]{2,1,0:T(8,128)S(1)} %get-tuple-element.12), custom_call_target="InvertDiagBlocksLowerTriangular" | custom-call | tf_op jit(solution)/shard_map/jit(_cho_solve)/triangular_solve | solution.py:15
  549.5 65.3 %psum.66 = f32[256]{0:T(256)S(1)} all-reduce(f32[256]{0:T(256)S(1)} %multiply_reduce_fusion.2), channel_id=1, replica_groups=mesh['ia'=4,'ja'=16,'ka'=2] {'ia','ja','ka'}, use_global_device_ids=true, to_apply=%region_9.11 | all-reduce | flops 256 | bytes 2048 | tf_op jit(solution)/shard_map/psum | solution.py:19
  616.6 77.4 %all-gather = bf16[32,6,256]{2,1,0:T(8,128)(2,1)S(1)} all-gather(bf16[1,6,256]{2,1,0:T(8,128)(2,1)S(1)} %get-tuple-element.83), channel_id=1, replica_groups=mesh['ia'=4,'ja'=16,'ka'=2] {'ja','ka'}, dimensions={0}, use_global_device_ids=true | all-gather | bytes 101376 | tf_op jit(solution)/shard_map/all_gather | solution.py:50
  699.2 58.2 %all-reduce.18.cloned.1.call-done = f32[256,256]{0,1:T(8,128)} async-done(((f32[256,256]{0,1:T(8,128)}), f32[256,256]{0,1:T(8,128)}) %all-reduce.18.cloned.1.call-update) | async-done | bytes 262160 | tf_op jit(solution)/shard_map/psum | solution.py:26
  758.6 11.7 cholesky.248
  780.7 11.7 cholesky.265
  799.3 19.7 %custom-call.37 = f32[2,128,128]{1,2,0:T(8,128)S(1)} custom-call(f32[2,128,128]{2,1,0:T(8,128)S(1)} %get-tuple-element.20), custom_call_target="InvertDiagBlocksLowerTriangular" | custom-call | tf_op jit(solution)/shard_map/jit(_cho_solve)/triangular_solve | solution.py:15
  821.5 63.3 %psum.68 = f32[256]{0:T(256)S(1)} all-reduce(f32[256]{0:T(256)S(1)} %multiply_reduce_fusion.1), channel_id=1, replica_groups=mesh['ia'=4,'ja'=16,'ka'=2] {'ia','ja','ka'}, use_global_device_ids=true, to_apply=%region_13.15 | all-reduce | flops 256 | bytes 2048 | tf_op jit(solution)/shard_map/psum | solution.py:19
  886.7 26.1 %all_gather.7 = bf16[64,256]{1,0:T(8,128)(2,1)S(1)} all-gather(bf16[8,256]{1,0:T(8,128)(2,1)S(1)} %get-tuple-element.109), channel_id=1, replica_groups=mesh['ia'=4,'ja'=16,'ka'=2] {'ia','ka'}, dimensions={0}, use_global_device_ids=true | all-gather | bytes 36864 | tf_op jit(solution)/shard_map/all_gather | solution.py:61
  922.5 11.7 cholesky.316
  944.6 11.7 cholesky.333
  963.2 19.8 %custom-call.39 = f32[2,128,128]{1,2,0:T(8,128)S(1)} custom-call(f32[2,128,128]{2,1,0:T(8,128)S(1)} %get-tuple-element.36), custom_call_target="InvertDiagBlocksLowerTriangular" | custom-call | tf_op jit(solution)/shard_map/jit(_cho_solve)/triangular_solve | solution.py:15
  983.1 45.0 %all-reduce.20.cloned.1.call-done = f32[256,256]{0,1:T(8,128)} async-done(((f32[256,256]{0,1:T(8,128)}), f32[256,256]{0,1:T(8,128)}) %all-reduce.20.cloned.1.call-update) | async-done | bytes 262160 | tf_op jit(solution)/shard_map/psum | solution.py:26
  1051.3 11.7 cholesky.299
  1070.0 19.9 %custom-call.38 = f32[2,128,128]{1,2,0:T(8,128)S(1)} custom-call(f32[2,128,128]{2,1,0:T(8,128)S(1)} %get-tuple-element.28), custom_call_target="InvertDiagBlocksLowerTriangular" | custom-call | tf_op jit(solution)/shard_map/jit(_cho_solve)/triangular_solve | solution.py:15
  1089.9 421.6 %all-reduce.22.cloned.1.call-done = f32[128,256]{0,1:T(8,128)} async-done(((f32[128,256]{0,1:T(8,128)}), f32[128,256]{0,1:T(8,128)}) %all-reduce.22.cloned.1.call-update) | async-done | bytes 131088
  1513.8 22.0 %reduce-scatter.8.cloned.1.call-done = f32[128,256]{0,1:T(8,128)} async-done(((f32[512,256]{0,1:T(8,128)}), f32[128,256]{0,1:T(8,128)}) %reduce-scatter.8.cloned.1.call-update) | async-done | bytes 131088 | tf_op jit(solution)/shard_map/reduce_scatter | solution.py:76
  1539.1 65.8 %all-reduce.4 = (f32[256]{0:T(256)S(1)}, f32[256]{0:T(256)S(1)}) all-reduce(f32[256]{0:T(256)S(1)} %multiply_reduce_fusion.3, f32[256]{0:T(256)S(1)} %multiply_reduce_fusion), channel_id=1, replica_groups=mesh['ia'=4,'ja'=16,'ka'=2] {'ia','ja','ka'}, use_global_device_ids=true, to_apply=%region_17.19 | all-reduce | flops 512 | bytes 4096 | tf_op jit(solution)/shard_map/psum | solution.py:19
  (188 shorter events, 159.9 us)
Async XLA Ops:
  7.2 11.4 copy-start
  7.2 335.9 %all-reduce.16.cloned.1.call-start = ((), (), s32[]{:S(2)}) async-start(), calls=%async_computation.4 | async-start | bytes 524288 | tf_op jit(solution)/shard_map/psum | solution.py:40
  10.2 442.1 %all-reduce.12.cloned.1.call-start = ((), (), s32[]{:S(2)}) async-start(), calls=%async_computation.2 | async-start | bytes 524288 | tf_op jit(solution)/shard_map/psum | solution.py:38
  12.3 474.5 %all-reduce.14.cloned.1.call-start = ((), (), s32[]{:S(2)}) async-start(), calls=%async_computation.3 | async-start | bytes 524288 | tf_op jit(solution)/shard_map/psum | solution.py:39
  14.5 4.0 copy-start.1
  14.5 114.2 %copy-start.5 = (u32[128]{0:T(128)S(1)}, u32[128]{0:T(128)}, u32[]{:S(2)}) copy-start(u32[128]{0:T(128)} %constant.199) | copy-start | bytes 1540
  14.5 115.4 %copy-start.6 = (u32[128]{0:T(128)S(1)}, u32[128]{0:T(128)}, u32[]{:S(2)}) copy-start(u32[128]{0:T(128)} %constant.203) | copy-start | bytes 1540
  14.5 742.9 %all-reduce.18.cloned.1.call-start = ((), (), s32[]{:S(2)}) async-start(), calls=%async_computation.5 | async-start | bytes 524288 | tf_op jit(solution)/shard_map/psum | solution.py:26
  105.5 14.6 collective-permute-start.6
  106.8 17.8 %collective-permute-start.5 = (f32[8,256]{1,0:T(8,128)S(1)}, f32[8,256]{1,0:T(8,128)S(1)}, u32[]{:S(2)}, u32[]{:S(2)}) collective-permute-start(f32[8,256]{1,0:T(8,128)S(1)} %fusion), channel_id=1, source_target_pairs={{0,6},{1,7},{2,8},{3,9},{4,10},{5,11},{6,12},{7,13},{8,14},{9,15},... | collective-permute-start | bytes 24584
  108.1 10.7 collective-permute-start.7
  109.4 21.7 %collective-permute-start.4 = (f32[8,256]{1,0:T(8,128)S(1)}, f32[8,256]{1,0:T(8,128)S(1)}, u32[]{:S(2)}, u32[]{:S(2)}) collective-permute-start(f32[8,256]{1,0:T(8,128)S(1)} %fusion), channel_id=1, source_target_pairs={{0,5},{1,6},{2,7},{3,8},{4,9},{5,10},{6,11},{7,12},{8,13},{9,14},{... | collective-permute-start | bytes 24584
  110.7 20.5 %collective-permute-start.3 = (f32[8,256]{1,0:T(8,128)S(1)}, f32[8,256]{1,0:T(8,128)S(1)}, u32[]{:S(2)}, u32[]{:S(2)}) collective-permute-start(f32[8,256]{1,0:T(8,128)S(1)} %fusion), channel_id=1, source_target_pairs={{0,4},{1,5},{2,6},{3,7},{4,8},{5,9},{6,10},{7,11},{8,12},{9,13},{1... | collective-permute-start | bytes 24584
  118.8 12.4 collective-permute-start.2
  120.1 11.1 collective-permute-start.1
  124.7 6.6 collective-permute-start
  488.0 206.1 %copy-start.4 = (f32[128,256]{1,0:T(8,128)S(1)}, f32[128,256]{1,0:T(8,128)}, u32[]{:S(2)}) copy-start(f32[128,256]{1,0:T(8,128)} %param.9) | copy-start | bytes 393220
  616.6 202.4 %reduce-scatter.6.cloned.1.call-start = ((), (), s32[]{:S(2)}) async-start(), calls=%async_computation.6 | async-start | bytes 73728 | tf_op jit(solution)/shard_map/reduce_scatter | solution.py:57
  694.1 63.3 %copy-start.3 = (f32[256,256]{0,1:T(8,128)S(1)}, f32[256,256]{0,1:T(8,128)}, u32[]{:S(2)}) copy-start(f32[256,256]{0,1:T(8,128)} %all-reduce.14.cloned.1.call-done) | copy-start | bytes 786436
  699.0 329.1 %all-reduce.20.cloned.1.call-start = ((), (), s32[]{:S(2)}) async-start(), calls=%async_computation.7 | async-start | bytes 524288 | tf_op jit(solution)/shard_map/psum | solution.py:26
  886.6 624.9 %all-reduce.22.cloned.1.call-start = ((), (), s32[]{:S(2)}) async-start(), calls=%async_computation.9 | async-start | bytes 262144
  912.8 9.6 copy-start.2
  920.8 614.9 %reduce-scatter.8.cloned.1.call-start = ((), (), s32[]{:S(2)}) async-start(), calls=%async_computation.8 | async-start | bytes 655360 | tf_op jit(solution)/shard_map/reduce_scatter | solution.py:76
Sparse Core Ops, SparseCore 0:
  10.4 332.5 all-reduce.15
  346.2 106.0 all-reduce.11
  454.8 32.0 all-reduce.13
  616.7 140.6 all-reduce.17
  760.2 32.6 reduce-scatter.5
  886.7 141.2 all-reduce.19
  1031.1 480.3 all-reduce.21
  1513.9 21.8 reduce-scatter.7
where the time goes:
time: 1620 us; the launch traced here: 1610 us
  waiting for transfers between devices  902 us (56%)
  blocking collectives  385 us (24%)
  other arithmetic  223 us (14%)
  matrix products  37.3 us (2%)
  starting transfers between devices  23.9 us (1%)
  between operations  21.7 us (1%)
  local copies, waits for them, and re-layouts  20.6 us (1%)
    unnamed x17, waiting for transfers between devices  422 us
    psum x1, waiting for transfers between devices, body(): gram_column = lax.psum(gram_of(column_in), ('ja', 'ka'))  211 us
    psum x3, blocking collectives, column_norms(): squares = lax.psum(jnp.sum(unscaled * unscaled, axis=0), ('ia', 'ja', 'ka'))  194 us
    another operation x27, other arithmetic, solve_rows(): lower_factor = jnp.linalg.cholesky(system)  138 us
    psum x1, waiting for transfers between devices, body(): gram_second = lax.psum(gram_of(second_in), 'ja')  109 us
    psum x2, waiting for transfers between devices, normalize(): return (scaled, lax.psum(gram_of(scaled), ('ia', 'ja', 'ka')))  103 us
    unnamed x1, blocking collectives  86.8 us
    another operation x9, other arithmetic, solve_rows(): return jax.scipy.linalg.cho_solve((lower_factor, True), right_side.T).T  79.7 us
  transfers between devices with their start and end apart: 16, of which 7 were waited for; matrix products, arithmetic and copies ran while one was open for 18% of the time, Pallas kernels for 0%

commit v1 on v0

v1 whole, which is shorter than its diff:
```python
import jax
import jax.numpy as jnp
from jax import lax
from jax.sharding import PartitionSpec as P

ALL = ("ia", "ja", "ka")
HI = lax.Precision.HIGHEST


def gram_of(factor):
    return lax.dot_general(
        factor, factor, (((0,), (0,)), ((), ())), precision=HI, preferred_element_type=jnp.float32
    )


def matmul(left, right):
    return jnp.dot(left, right, precision=HI, preferred_element_type=jnp.float32)


def inverse_factor(system):
    lower = jnp.linalg.cholesky(system)
    eye = jnp.eye(system.shape[0], dtype=jnp.float32)
    return lax.linalg.triangular_solve(lower, eye, left_side=True, lower=True)


def solve_rows(right_side, factor):
    return matmul(matmul(right_side, factor.T), factor)


def exchange(blocks, axes):
    return lax.all_to_all(blocks, axes, 0, 0, tiled=True)


def reduce_rows(whole, axes, parts):
    rows, width = whole.shape
    return jnp.sum(exchange(whole.reshape(parts, rows // parts, width), axes), axis=0)


def gather_rows(rows, axes, parts):
    return exchange(jnp.broadcast_to(rows[None], (parts,) + rows.shape), axes)


def column_scale(unscaled, row_total):
    return lax.rsqrt(jnp.sum(unscaled * unscaled, axis=0) / row_total + 1e-06)


def body(tensor, matrix, second_in, third_in, column_in):
    span_first, span_second, span_third = tensor.shape
    span_column = matrix.shape[1]
    rank = second_in.shape[1]
    n_ia, n_ja, n_ka = (lax.axis_size(a) for a in ALL)
    n_all = n_ia * n_ja * n_ka
    n_jk = n_ja * n_ka
    at_ia, at_ja, at_ka = (lax.axis_index(a) for a in ALL)
    at = (at_ia * n_ja + at_ja) * n_ka + at_ka

    part_second = span_second // n_ka
    part_third = span_third // n_ja
    slab = rank // n_ia
    grams = [
        gram_of(lax.dynamic_slice_in_dim(second_in, at_ka * part_second, part_second, 0)),
        gram_of(lax.dynamic_slice_in_dim(third_in, at_ja * part_third, part_third, 0)),
        gram_of(column_in),
    ]
    slabs = [
        lax.dynamic_slice_in_dim(g, at_ia * slab, slab, 0).reshape(n_jk, slab // n_jk, rank)
        for g in grams
    ]
    per = slab // n_jk
    sums = jnp.sum(exchange(jnp.concatenate(slabs, axis=1), ("ja", "ka")), axis=0)
    gs, gt, gc = sums[:per], sums[per : 2 * per], sums[2 * per :]
    gathered = gather_rows(jnp.concatenate([gs * gt + gc, gt], axis=0), ALL, n_all)
    system_one = gathered[:, :per].reshape(rank, rank)
    gram_third = gathered[:, per:].reshape(rank, rank)

    column_half = column_in.astype(jnp.bfloat16)
    weights_one = (second_in[:, None, :] * third_in[None, :, :]).astype(jnp.bfloat16)
    weights_one = lax.optimization_barrier(weights_one.reshape(span_second * span_third, rank))
    flat = lax.optimization_barrier(tensor.reshape(span_first, span_second * span_third))
    first_whole = jnp.dot(flat, weights_one, preferred_element_type=jnp.float32)
    first_whole = first_whole + jnp.dot(matrix, column_half, preferred_element_type=jnp.float32)
    rows_one = reduce_rows(first_whole, ("ja", "ka"), n_jk)
    partial_one = gather_rows(rows_one, ALL, n_all).reshape(span_first * n_ia, rank)
    raw_one = solve_rows(partial_one, inverse_factor(system_one))
    first_new = raw_one * column_scale(raw_one, span_first * n_ia)
    gram_first = gram_of(first_new)
    per_first = span_first // n_jk
    first_out = lax.dynamic_slice_in_dim(first_new, at * per_first, per_first, 0)
    first_half = lax.dynamic_slice_in_dim(first_new, at_ia * span_first, span_first, 0).astype(
        jnp.bfloat16
    )

    weights_two = (first_half.astype(jnp.float32)[:, None, :] * third_in[None, :, :]).astype(
        jnp.bfloat16
    )
    second_whole = lax.dot_general(
        tensor, weights_two, (((0, 2), (0, 1)), ((), ())), preferred_element_type=jnp.float32
    )
    n_ik = n_ia * n_ka
    per_second = span_second // n_ik
    rows_two = reduce_rows(second_whole, ("ia", "ka"), n_ik)
    partial_two = gather_rows(rows_two, ALL, n_all).reshape(n_all * per_second, rank)
    raw_two = solve_rows(partial_two, inverse_factor(gram_first * gram_third))
    second_new = raw_two * column_scale(raw_two, span_second * n_ja)
    gram_updated = gram_of(second_new)
    second_out = lax.dynamic_slice_in_dim(second_new, at * per_second, per_second, 0)
    blocks = second_new.reshape(n_ia, n_ja, n_ka, per_second, rank)
    second_half = (
        lax.dynamic_index_in_dim(blocks, at_ja, 1, keepdims=False)
        .reshape(span_second, rank)
        .astype(jnp.bfloat16)
    )

    weights_three = (first_half[:, None, :] * second_half[None, :, :]).reshape(
        span_first * span_second, rank
    )
    third_whole = lax.dot_general(
        tensor.reshape(span_first * span_second, span_third),
        weights_three,
        (((0,), (0,)), ((), ())),
        preferred_element_type=jnp.float32,
    )
    column_whole = lax.dot_general(
        matrix, first_half, (((0,), (0,)), ((), ())), preferred_element_type=jnp.float32
    )
    rows_column = reduce_rows(column_whole, "ia", n_ia)
    raw_column = solve_rows(rows_column, inverse_factor(gram_first))
    squares = jnp.sum(raw_column * raw_column, axis=0, keepdims=True)
    n_ij = n_ia * n_ja
    per_third = span_third // n_ij
    rows_three = reduce_rows(third_whole, ("ia", "ja"), n_ij)
    last = gather_rows(jnp.concatenate([rows_three, squares], axis=0), ALL, n_all)
    partial_three = last[:, :per_third].reshape(n_all * per_third, rank)
    raw_three = solve_rows(partial_three, inverse_factor(gram_first * gram_updated))
    third_new = raw_three * column_scale(raw_three, span_third * n_ka)
    third_out = lax.dynamic_slice_in_dim(third_new, at * per_third, per_third, 0)
    column_squares = jnp.sum(last[:, per_third], axis=0)
    column_out = raw_column * lax.rsqrt(column_squares / (span_column * n_jk) + 1e-06)
    return (first_out, second_out[None], third_out[None], column_out[None])


def solution(mesh):
    placed = (
        P("ia", "ja", "ka"),
        P("ia", ("ja", "ka")),
        P("ja", None),
        P("ka", None),
        P(("ja", "ka"), None),
    )
    return jax.shard_map(
        body,
        mesh=mesh,
        in_specs=placed,
        out_specs=(
            P(("ia", "ja", "ka"), None),
            P("ja", ("ia", "ka"), None),
            P("ka", ("ia", "ja"), None),
            P(("ja", "ka"), "ia", None),
        ),
        check_vma=False,
    )
```

time: 1620 us -> 419 us (0.26)
  waiting for transfers between devices: 902 us -> 60.9 us
  blocking collectives: 385 us -> 0 us
  starting transfers between devices: 23.9 us -> 61.2 us
    psum x5 -> x0, waiting for transfers between devices: 458 us -> none  [the longest x1 211 us: body(): gram_column = lax.psum(gram_of(column_in), ('ja', 'ka'))]
    unnamed x17 -> x0, waiting for transfers between devices: 422 us -> none
    psum x3 -> x0, blocking collectives: 194 us -> none  [column_norms(): squares = lax.psum(jnp.sum(unscaled * unscaled, axis=0), ('ia', 'ja', 'ka'))]
    all_gather x2 -> x0, blocking collectives: 103 us -> none  [the longest x1 77.4 us: body(): lax.all_gather(first_new.astype(jnp.bfloat16), ('ja', 'ka'), axis=0, tile...]
    unnamed x1 -> x0, blocking collectives: 86.8 us -> none
    all_to_all x0 -> x9, starting transfers between devices: none -> 61.2 us  [exchange(): return lax.all_to_all(blocks, axes, 0, 0, tiled=True)]
    all_to_all x0 -> x9, waiting for transfers between devices: none -> 60.9 us  [exchange(): return lax.all_to_all(blocks, axes, 0, 0, tiled=True)]
    unnamed x9 -> x0, starting transfers between devices: 23.1 us -> none
  transfers between devices with their start and end apart: 16 -> 9, of which waited for: 7 -> 6; matrix products, arithmetic and copies ran while one was open for 18% -> 62% of each run, Pallas kernels for 0% -> 0%
where the time goes in v1:
time: 419 us; the launch traced here: 411 us
  other arithmetic  224 us (53%)
  starting transfers between devices  61.2 us (15%)
  waiting for transfers between devices  60.9 us (15%)
  matrix products  29.5 us (7%)
  local copies, waits for them, and re-layouts  28 us (7%)
  between operations  7.27 us (2%)
    another operation x28, other arithmetic, inverse_factor(): lower = jnp.linalg.cholesky(system)  138 us
    another operation x9, other arithmetic, inverse_factor(): return lax.linalg.triangular_solve(lower, eye, left_side=True, lower=True)  80 us
    all_to_all x9, starting transfers between devices, exchange(): return lax.all_to_all(blocks, axes, 0, 0, tiled=True)  61.2 us
    all_to_all x9, waiting for transfers between devices, exchange(): return lax.all_to_all(blocks, axes, 0, 0, tiled=True)  60.9 us
    another operation x29, local copies, waits for them, and re-layouts, inverse_factor(): return lax.linalg.triangular_solve(lower, eye, left_side=True, lower=True)  15.9 us
  transfers between devices with their start and end apart: 9, of which 6 were waited for; matrix products, arithmetic and copies ran while one was open for 62% of the time, Pallas kernels for 0%

profile of v1, /device:TPU:1, one launch (start us, length us, event | category | flops | bytes accessed | tf_op | source)
XLA Modules:
  0.0 410.8 jit_solution(6013422801636860420)
XLA Ops:
  6.4 11.3 %all-to-all-start.2 = ((f32[32,6,256]{2,1,0:T(8,128)}), f32[32,6,256]{2,1,0:T(8,128)S(1)}, u32[]{:S(2)}, u32[]{:S(2)}) async-start(f32[32,6,256]{2,1,0:T(8,128)} %pad_maximum_fusion), calls=%async_computation.2 | async-start | bytes 524288 | tf_op jit(solution)/shard_map/all_to_all | solution.py:31
  34.4 9.8 %all-to-all-done = f32[32,6,256]{2,1,0:T(8,128)S(1)} async-done(((f32[32,6,256]{2,1,0:T(8,128)}), f32[32,6,256]{2,1,0:T(8,128)S(1)}, u32[]{:S(2)}, u32[]{:S(2)}) %all-to-all-start) | async-done | bytes 196640 | tf_op jit(solution)/shard_map/all_to_all | solution.py:31
  51.1 13.7 %all-to-all-done.3 = f32[128,4,256]{2,1,0:T(4,128)S(1)} async-done(((f32[128,4,256]{2,1,0:T(4,128)}), f32[128,4,256]{2,1,0:T(4,128)S(1)}, u32[]{:S(2)}, u32[]{:S(2)}) %all-to-all-start.3) | async-done | bytes 524320 | tf_op jit(solution)/shard_map/all_to_all | solution.py:31
  71.4 11.7 %cholesky.214 = f32[128,128]{1,0:T(8,128)S(1)} custom-call(f32[128,128]{1,0:T(8,128)S(1)} %cholesky.346), custom_call_target="Cholesky" | custom-call | tf_op jit(solution)/shard_map/jit(cholesky)/cholesky | solution.py:21
  83.2 9.8 %custom-call.17 = f32[1,128,128]{1,2,0:T(8,128)S(1)} custom-call(f32[1,128,128]{2,1,0:T(8,128)S(1)} %get-tuple-element.95), custom_call_target="InvertDiagBlocksLowerTriangular" | custom-call | tf_op jit(solution)/shard_map/jit(cholesky)/cholesky | solution.py:21
  93.5 11.7 %cholesky.231 = f32[128,128]{1,0:T(8,128)S(1)} custom-call(f32[128,128]{1,0:T(8,128)S(1)} %convolution_subtract_fusion.7), custom_call_target="Cholesky" | custom-call | tf_op jit(solution)/shard_map/jit(cholesky)/cholesky | solution.py:21
  111.9 20.1 %custom-call.18 = f32[2,128,128]{1,2,0:T(8,128)S(1)} custom-call(f32[2,128,128]{2,1,0:T(8,128)S(1)} %get-tuple-element.32), custom_call_target="InvertDiagBlocksLowerTriangular" | custom-call | tf_op jit(solution)/shard_map/triangular_solve/custom-call.0 | solution.py:23
  145.0 11.7 %cholesky.248 = f32[128,128]{1,0:T(8,128)S(1)} custom-call(f32[128,128]{1,0:T(8,128)S(1)} %cholesky.349), custom_call_target="Cholesky" | custom-call | tf_op jit(solution)/shard_map/jit(cholesky)/cholesky | solution.py:21
  156.8 9.8 %custom-call.19 = f32[1,128,128]{1,2,0:T(8,128)S(1)} custom-call(f32[1,128,128]{2,1,0:T(8,128)S(1)} %get-tuple-element.91), custom_call_target="InvertDiagBlocksLowerTriangular" | custom-call | tf_op jit(solution)/shard_map/jit(cholesky)/cholesky | solution.py:21
  167.0 11.7 %cholesky.265 = f32[128,128]{1,0:T(8,128)S(1)} custom-call(f32[128,128]{1,0:T(8,128)S(1)} %convolution_subtract_fusion.6), custom_call_target="Cholesky" | custom-call | tf_op jit(solution)/shard_map/jit(cholesky)/cholesky | solution.py:21
  185.4 20.1 %custom-call.20 = f32[2,128,128]{1,2,0:T(8,128)S(1)} custom-call(f32[2,128,128]{2,1,0:T(8,128)S(1)} %get-tuple-element.33), custom_call_target="InvertDiagBlocksLowerTriangular" | custom-call | tf_op jit(solution)/shard_map/triangular_solve/custom-call.0 | solution.py:23
  206.1 11.7 %cholesky.282 = f32[128,128]{1,0:T(8,128)S(1)} custom-call(f32[128,128]{1,0:T(8,128)S(1)} %cholesky.352), custom_call_target="Cholesky" | custom-call | tf_op jit(solution)/shard_map/jit(cholesky)/cholesky | solution.py:21
  217.9 9.8 %custom-call.21 = f32[1,128,128]{1,2,0:T(8,128)S(1)} custom-call(f32[1,128,128]{2,1,0:T(8,128)S(1)} %get-tuple-element.87), custom_call_target="InvertDiagBlocksLowerTriangular" | custom-call | tf_op jit(solution)/shard_map/jit(cholesky)/cholesky | solution.py:21
  228.2 11.7 %cholesky.299 = f32[128,128]{1,0:T(8,128)S(1)} custom-call(f32[128,128]{1,0:T(8,128)S(1)} %convolution_subtract_fusion.5), custom_call_target="Cholesky" | custom-call | tf_op jit(solution)/shard_map/jit(cholesky)/cholesky | solution.py:21
  247.7 19.8 %custom-call.22 = f32[2,128,128]{1,2,0:T(8,128)S(1)} custom-call(f32[2,128,128]{2,1,0:T(8,128)S(1)} %get-tuple-element.34), custom_call_target="InvertDiagBlocksLowerTriangular" | custom-call | tf_op jit(solution)/shard_map/triangular_solve/custom-call.0 | solution.py:23
  271.7 7.2 %all-to-all-done.7 = f32[4,128,256]{1,2,0:T(8,128)S(1)} async-done(((f32[4,128,256]{1,2,0:T(8,128)}), f32[4,128,256]{1,2,0:T(8,128)S(1)}, u32[]{:S(2)}, u32[]{:S(2)}) %all-to-all-start.7) | async-done | bytes 524320 | tf_op jit(solution)/shard_map/all_to_all | solution.py:31
  279.9 10.7 %all-to-all-start.5 = ((f32[128,8,256]{2,1,0:T(8,128)}), f32[128,8,256]{2,1,0:T(8,128)S(1)}, u32[]{:S(2)}, u32[]{:S(2)}) async-start(f32[128,8,256]{2,1,0:T(8,128)} %broadcast_in_dim.19), calls=%async_computation.5 | async-start | bytes 2097152 | tf_op jit(solution)/shard_map/all_to_all | solution.py:31
  294.9 15.1 %all-to-all-done.5 = f32[128,8,256]{2,1,0:T(8,128)S(1)} async-done(((f32[128,8,256]{2,1,0:T(8,128)}), f32[128,8,256]{2,1,0:T(8,128)S(1)}, u32[]{:S(2)}, u32[]{:S(2)}) %all-to-all-start.5) | async-done | bytes 1048608 | tf_op jit(solution)/shard_map/all_to_all | solution.py:31
  324.5 11.7 %cholesky.316 = f32[128,128]{1,0:T(8,128)S(1)} custom-call(f32[128,128]{1,0:T(8,128)S(1)} %cholesky.355), custom_call_target="Cholesky" | custom-call | tf_op jit(solution)/shard_map/jit(cholesky)/cholesky | solution.py:21
  336.3 9.8 %custom-call.23 = f32[1,128,128]{1,2,0:T(8,128)S(1)} custom-call(f32[1,128,128]{2,1,0:T(8,128)S(1)} %get-tuple-element.83), custom_call_target="InvertDiagBlocksLowerTriangular" | custom-call | tf_op jit(solution)/shard_map/jit(cholesky)/cholesky | solution.py:21
  346.6 11.7 %cholesky.333 = f32[128,128]{1,0:T(8,128)S(1)} custom-call(f32[128,128]{1,0:T(8,128)S(1)} %convolution_subtract_fusion.4), custom_call_target="Cholesky" | custom-call | tf_op jit(solution)/shard_map/jit(cholesky)/cholesky | solution.py:21
  365.0 19.9 %custom-call.24 = f32[2,128,128]{1,2,0:T(8,128)S(1)} custom-call(f32[2,128,128]{2,1,0:T(8,128)S(1)} %get-tuple-element.35), custom_call_target="InvertDiagBlocksLowerTriangular" | custom-call | tf_op jit(solution)/shard_map/triangular_solve/custom-call.0 | solution.py:23
  386.2 7.9 %all-to-all-start.8 = ((f32[128,3,256]{2,1,0:T(4,128)}), f32[128,3,256]{2,1,0:T(4,128)S(1)}, u32[]{:S(2)}, u32[]{:S(2)}) async-start(f32[128,3,256]{2,1,0:T(4,128)} %broadcast_in_dim.22), calls=%async_computation.8 | async-start | bytes 1048576 | tf_op jit(solution)/shard_map/all_to_all | solution.py:31
  395.3 12.4 %all-to-all-done.8 = f32[128,3,256]{2,1,0:T(4,128)S(1)} async-done(((f32[128,3,256]{2,1,0:T(4,128)}), f32[128,3,256]{2,1,0:T(4,128)S(1)}, u32[]{:S(2)}, u32[]{:S(2)}) %all-to-all-start.8) | async-done | bytes 393248 | tf_op jit(solution)/shard_map/all_to_all | solution.py:31
  (185 shorter events, 118.3 us)
Async XLA Ops:
  0.6 23.4 %copy-start = (bf16[192,512]{1,0:T(8,128)(2,1)S(1)}, bf16[192,512]{1,0:T(8,128)(2,1)}, u32[]{:S(2)}) copy-start(bf16[192,512]{1,0:T(8,128)(2,1)} %param.9) | copy-start | bytes 589828
  6.4 21.4 %all-to-all-start.2 = ((f32[32,6,256]{2,1,0:T(8,128)}), f32[32,6,256]{2,1,0:T(8,128)S(1)}, u32[]{:S(2)}, u32[]{:S(2)}) async-start(f32[32,6,256]{2,1,0:T(8,128)} %pad_maximum_fusion), calls=%async_computation.2 | async-start | bytes 524288 | tf_op jit(solution)/shard_map/all_to_all | solution.py:31
  17.7 2.5 copy-start.2
  23.1 1.0 copy-start.1
  27.8 16.4 %all-to-all-start = ((f32[32,6,256]{2,1,0:T(8,128)}), f32[32,6,256]{2,1,0:T(8,128)S(1)}, u32[]{:S(2)}, u32[]{:S(2)}) async-start(f32[32,6,256]{2,1,0:T(8,128)} %reshape.111), calls=%async_computation | async-start | bytes 524288 | tf_op jit(solution)/shard_map/all_to_all | solution.py:31
  45.0 19.8 %all-to-all-start.3 = ((f32[128,4,256]{2,1,0:T(4,128)}), f32[128,4,256]{2,1,0:T(4,128)S(1)}, u32[]{:S(2)}, u32[]{:S(2)}) async-start(f32[128,4,256]{2,1,0:T(4,128)} %broadcast_in_dim.18), calls=%async_computation.3 | async-start | bytes 1048576 | tf_op jit(solution)/shard_map/all_to_all | solution.py:31
  65.9 67.4 %all-to-all-start.1 = ((f32[128,6,256]{2,1,0:T(8,128)}), f32[128,6,256]{2,1,0:T(8,128)S(1)}, u32[]{:S(2)}, u32[]{:S(2)}) async-start(f32[128,6,256]{2,1,0:T(8,128)} %broadcast_in_dim.17), calls=%async_computation.1 | async-start | bytes 2097152 | tf_op jit(solution)/shard_map/all_to_all | solution.py:31
  133.4 3.2 copy-start.3
  133.4 3.2 copy-start.9
  136.6 110.0 %copy-start.7 = (bf16[192,256]{1,0:T(8,128)(2,1)}, bf16[192,256]{1,0:T(8,128)(2,1)S(1)}, u32[]{:S(2)}) copy-start(bf16[192,256]{1,0:T(8,128)(2,1)S(1)} %get-tuple-element.69) | copy-start | bytes 294916
  139.5 128.0 %all-to-all-start.4 = ((f32[8,8,256]{2,1,0:T(8,128)}), f32[8,8,256]{2,1,0:T(8,128)S(1)}, u32[]{:S(2)}, u32[]{:S(2)}) async-start(f32[8,8,256]{2,1,0:T(8,128)} %fusion.13), calls=%async_computation.4 | async-start | bytes 131072 | tf_op jit(solution)/shard_map/all_to_all | solution.py:31
  246.6 21.0 %copy-start.5 = (f32[256,256]{1,0:T(8,128)}, f32[256,256]{1,0:T(8,128)S(1)}, u32[]{:S(2)}) copy-start(f32[256,256]{1,0:T(8,128)S(1)} %get-tuple-element.298) | copy-start | bytes 786436
  267.5 12.4 %copy-start.10 = (f32[2,128,128]{1,2,0:T(8,128)}, f32[2,128,128]{1,2,0:T(8,128)S(1)}, u32[]{:S(2)}) copy-start(f32[2,128,128]{1,2,0:T(8,128)S(1)} %custom-call.22) | copy-start | bytes 393220
  267.5 11.3 %all-to-all-start.7 = ((f32[4,128,256]{1,2,0:T(8,128)}), f32[4,128,256]{1,2,0:T(8,128)S(1)}, u32[]{:S(2)}, u32[]{:S(2)}) async-start(f32[4,128,256]{1,2,0:T(8,128)} %bitcast.153), calls=%async_computation.7 | async-start | bytes 1048576 | tf_op jit(solution)/shard_map/all_to_all | solution.py:31
  279.9 30.1 %all-to-all-start.5 = ((f32[128,8,256]{2,1,0:T(8,128)}), f32[128,8,256]{2,1,0:T(8,128)S(1)}, u32[]{:S(2)}, u32[]{:S(2)}) async-start(f32[128,8,256]{2,1,0:T(8,128)} %broadcast_in_dim.19), calls=%async_computation.5 | async-start | bytes 2097152 | tf_op jit(solution)/shard_map/all_to_all | solution.py:31
  294.9 19.1 %copy-start.8 = (bf16[192,256]{1,0:T(8,128)(2,1)S(1)}, bf16[192,256]{1,0:T(8,128)(2,1)}, u32[]{:S(2)}) copy-start(bf16[192,256]{1,0:T(8,128)(2,1)} %copy-done.7) | copy-start | bytes 294916
  310.0 4.0 copy-start.4
  319.0 66.2 %all-to-all-start.6 = ((f32[64,2,256]{2,1,0:T(2,128)}), f32[64,2,256]{2,1,0:T(2,128)S(1)}, u32[]{:S(2)}, u32[]{:S(2)}) async-start(f32[64,2,256]{2,1,0:T(2,128)} %reshape.121), calls=%async_computation.6 | async-start | bytes 262144 | tf_op jit(solution)/shard_map/all_to_all | solution.py:31
  324.5 84.6 %copy-start.6 = (f32[128,256]{1,0:T(8,128)S(1)}, f32[128,256]{1,0:T(8,128)}, u32[]{:S(2)}) copy-start(f32[128,256]{1,0:T(8,128)} %get-tuple-element.109) | copy-start | bytes 393220
  386.2 21.5 %all-to-all-start.8 = ((f32[128,3,256]{2,1,0:T(4,128)}), f32[128,3,256]{2,1,0:T(4,128)S(1)}, u32[]{:S(2)}, u32[]{:S(2)}) async-start(f32[128,3,256]{2,1,0:T(4,128)} %broadcast_in_dim.22), calls=%async_computation.8 | async-start | bytes 1048576 | tf_op jit(solution)/shard_map/all_to_all | solution.py:31
